TPU v7x, 256 devices: a whole 4x4x8 slice. The times are simulated.
256 devices in a mesh: sec: 8 (over z_lo, core), ctx: 32 (over z_hi, x, y).
Axes of the slice: x: 4, y: 4, z: 8 (z_hi: 2, z_lo: 4; z = z_hi * 4 + z_lo), core: 2. Of those that a mesh axis runs over, the one named last changes fastest.
Arguments:
- q_frames: bfloat16 [8, 512, 8, 3584], P('sec', 'ctx'), may hold values from -8 to 8
- k_frames: bfloat16 [8, 512, 8, 512], P('sec', 'ctx'), may hold values from -8 to 8
- v_frames: bfloat16 [8, 512, 8, 512], P('sec', 'ctx'), may hold values from -6 to 6
- video_frames: int32 [8], replicated, may hold values from 256 to 512, as said below
- frame_section: int32 [8, 512], P('sec', 'ctx'), may hold values from 0 to 7, as said below
- frame_offset: int32 [8, 512], P('sec', 'ctx'), may hold values from 0 to 4088, as said below
Outputs:
- attention_out: bfloat16 [8, 4096, 3584], P('sec', 'ctx')
Inputs may be any that keep to these rules, and one draw needn't show every extreme that they name: `video_frames`: at least one section's video fills all 512 slots. `frame_section`: every device holds exactly 2 frame slots for each section. `frame_offset`: A multiple of 8; it falls in the 128 positions of the section's device whose ctx index equals that of the slot's device; the slots of one section cover its positions once. Slots at positions of frames beyond the video's length are not part of it.
All inputs are finite; a program needn't handle non-finite values.
Results may differ from a plain program's by a relative error of at most 0.006.
Values may be sent and summed in bfloat16 or wider, within the bound.
No kernel may reach another device: no remote copies, remote signals or barrier semaphores. Data moves between devices by JAX's collectives and lax.ppermute only.
A program may use at most 128 MiB of HBM per device.

v0:
```python
import math
import jax
import jax.numpy as jnp
from jax import lax
from jax.sharding import PartitionSpec as P

HEAD_DIM = 128
floor_score = -1e30


def source_slots(target_slot):
    slot_count = target_slot.shape[0]
    slot_ids = jnp.arange(slot_count, dtype=jnp.int32)
    matches = (target_slot[:, None] == slot_ids[None, :]).astype(jnp.int32)
    return jnp.sum(slot_ids[:, None] * matches, axis=0)


def make_absorb(query_sets, live_len, kv_heads, head_dim, score_scale):

    def absorb(carry, kv_piece, piece_start):
        key_block, value_block = kv_piece
        key_count = key_block.shape[0]
        key_pos = jnp.arange(key_count, dtype=jnp.int32)
        key_rows = key_block.reshape(key_count, kv_heads, head_dim)
        value_rows = value_block.reshape(key_count, kv_heads, head_dim)
        result = []
        for (queries, first_pos), carry_state in zip(query_sets, carry):
            row_count = queries.shape[0]
            active = (
                (piece_start <= first_pos + row_count - 1)
                & (piece_start < live_len)
                & (first_pos < live_len)
            )

            def advance(old_state, queries=queries, first_pos=first_pos, row_count=row_count):
                run_max, weight_sum, accumulated = old_state
                query_pos = first_pos + jnp.arange(row_count, dtype=jnp.int32)
                scores = (
                    jnp.einsum(
                        "rkgd,nkd->kgrn", queries, key_rows, preferred_element_type=jnp.float32
                    )
                    * score_scale
                )
                visible = (key_pos[None, :] <= query_pos[:, None]) & (key_pos[None, :] < live_len)
                masked = jnp.where(visible, scores, floor_score)
                new_max = jnp.maximum(run_max, jnp.max(masked, axis=-1))
                weights = jnp.where(visible, jnp.exp(scores - new_max[..., None]), 0.0)
                weight_sum = jnp.sum(weights, axis=-1)
                mixed = jnp.einsum(
                    "kgrn,nkd->rkgd",
                    weights.astype(jnp.bfloat16),
                    value_rows,
                    preferred_element_type=jnp.float32,
                )
                accumulated = mixed
                return (new_max, weight_sum, accumulated)

            result.append(lax.cond(active, advance, lambda unchanged: unchanged, carry_state))
        return tuple(result)

    return absorb


def finish(carry_state, first_pos, row_count, live_len):
    run_max, weight_sum, accumulated = carry_state
    query_pos = first_pos + jnp.arange(row_count, dtype=jnp.int32)
    is_live = query_pos < live_len
    safe_sum = jnp.where(is_live[None, None, :], weight_sum, 1.0)
    mixed = accumulated / jnp.transpose(safe_sum, (2, 0, 1))[..., None]
    mixed = mixed.reshape(row_count, -1)
    return jnp.where(is_live[:, None], mixed, 0.0).astype(jnp.bfloat16)


def local(q_frames, k_frames, v_frames, video_frames, frame_section, frame_offset):
    sections = lax.axis_size("sec")
    frames_dev = q_frames.shape[1]
    frame_len = q_frames.shape[2]
    per_section = frames_dev // sections
    kv_width = k_frames.shape[3]
    q_width = q_frames.shape[3]
    head_dim = HEAD_DIM
    kv_heads = kv_width // head_dim
    group_size = q_width // kv_width
    my_section = lax.axis_index("sec")
    my_place = lax.axis_index("ctx")
    section_of = frame_section[0]
    offsets = frame_offset[0]
    slot_ids = jnp.arange(frames_dev, dtype=jnp.int32)
    earlier = (section_of[:, None] == section_of[None, :]) & (slot_ids[None, :] < slot_ids[:, None])
    rank_in = jnp.sum(earlier.astype(jnp.int32), axis=1)
    order = source_slots(section_of * per_section + rank_in)
    send_q = jnp.take(q_frames[0], order, axis=0).reshape(sections, per_section, frame_len, q_width)
    send_k = jnp.take(k_frames[0], order, axis=0).reshape(
        sections, per_section, frame_len, kv_width
    )
    send_v = jnp.take(v_frames[0], order, axis=0).reshape(
        sections, per_section, frame_len, kv_width
    )
    send_off = jnp.take(offsets, order, axis=0).reshape(sections, per_section)
    got_q, got_k, got_v, got_off = (
        lax.all_to_all(send_q, "sec", split_axis=0, concat_axis=0, tiled=True),
        lax.all_to_all(send_k, "sec", split_axis=0, concat_axis=0, tiled=True),
        lax.all_to_all(send_v, "sec", split_axis=0, concat_axis=0, tiled=True),
        lax.all_to_all(send_off, "sec", split_axis=0, concat_axis=0, tiled=True),
    )
    local_slot = got_off.reshape(frames_dev) // frame_len - my_place * frames_dev
    placing = source_slots(local_slot)
    row_count = frames_dev * frame_len
    local_q = jnp.take(got_q.reshape(frames_dev, frame_len, q_width), placing, axis=0).reshape(
        row_count, q_width
    )
    local_k = jnp.take(got_k.reshape(frames_dev, frame_len, kv_width), placing, axis=0).reshape(
        row_count, kv_width
    )
    local_v = jnp.take(got_v.reshape(frames_dev, frame_len, kv_width), placing, axis=0).reshape(
        row_count, kv_width
    )
    live_len = video_frames[my_section] * frame_len
    half_rows = row_count // 2
    base_pos = my_place * row_count
    lead_q = local_q[:half_rows]
    tail_q = local_q[half_rows:]
    first_set = (lead_q, base_pos)
    second_set = (tail_q, base_pos + half_rows)
    query_sets = []
    for queries, first_pos in (first_set, second_set):
        query_sets.append((queries.reshape(half_rows, kv_heads, group_size, head_dim), first_pos))
    empty_state = (
        jnp.full((kv_heads, group_size, half_rows), floor_score, jnp.float32),
        jnp.zeros((kv_heads, group_size, half_rows), jnp.float32),
        jnp.zeros((half_rows, kv_heads, group_size, head_dim), jnp.float32),
    )
    absorb = make_absorb(query_sets, live_len, kv_heads, head_dim, 1.0 / math.sqrt(head_dim))
    states = absorb(
        (empty_state, empty_state),
        (
            lax.all_gather(local_k, "ctx", axis=0, tiled=True),
            lax.all_gather(local_v, "ctx", axis=0, tiled=True),
        ),
        jnp.int32(0),
    )
    first_out = finish(states[0], first_set[1], half_rows, live_len)
    second_out = finish(states[1], second_set[1], half_rows, live_len)
    return jnp.concatenate([first_out, second_out], axis=0)[None]


def solution(mesh):
    placed = (
        P("sec", "ctx", None, None),
        P("sec", "ctx", None, None),
        P("sec", "ctx", None, None),
        P(),
        P("sec", "ctx"),
        P("sec", "ctx"),
    )
    return jax.shard_map(
        local, mesh=mesh, in_specs=placed, out_specs=P("sec", "ctx", None), check_vma=False
    )
```

profile of v0, /device:TPU:32, one launch (start us, length us, event | category | flops | bytes accessed | tf_op | source)
XLA Modules:
  0.0 373.2 jit_solution(9911036601801687669)
XLA Ops:
  6.5 0.9 convert_reduce_fusion
  7.5 0.7 multiply_add_fusion
  8.1 0.1 select_reduce_fusion.1
  8.2 0.1 reduce_sum.51
  8.3 1.3 gather_fusion
  9.6 0.1 gather.13
  9.7 0.6 and_select_fusion
  10.3 6.0 %all-to-all-start.1 = ((s32[8,1,2]{2,1,0:T(1,128)}), s32[8,1,2]{2,1,0:T(1,128)S(1)}, u32[]{:S(2)}, u32[]{:S(2)}) async-start(s32[8,1,2]{2,1,0:T(1,128)} %bitcast.13), calls=%async_computation.1 | async-start | bytes 8192 | tf_op jit(solution)/shard_map/all_to_all | solution.py:104
  16.4 1.5 gather_fusion.5
  17.8 1.5 gather_fusion.3
  19.3 0.8 broadcast_select_fusion.2
  20.1 0.3 all-to-all-done.1
  20.4 4.8 %all-to-all-start.2 = ((bf16[8,2,8,512]{3,2,1,0:T(8,128)(2,1)}), bf16[8,2,8,512]{3,2,1,0:T(8,128)(2,1)S(1)}, u32[]{:S(2)}, u32[]{:S(2)}) async-start(bf16[8,2,8,512]{3,2,1,0:T(8,128)(2,1)} %bitcast.18), calls=%async_computation.2 | async-start | bytes 262144 | tf_op jit(solution)/shard_map/all_to_all | solution.py:102
  25.2 0.6 broadcast.297
  25.8 0.6 reduce.3
  26.4 0.1 reshape.217
  26.5 0.1 select_reduce_fusion
  26.6 4.3 %all-to-all-done.2 = bf16[8,2,8,512]{3,2,1,0:T(8,128)(2,1)S(1)} async-done(((bf16[8,2,8,512]{3,2,1,0:T(8,128)(2,1)}), bf16[8,2,8,512]{3,2,1,0:T(8,128)(2,1)S(1)}, u32[]{:S(2)}, u32[]{:S(2)}) %all-to-all-start.2) | async-done | bytes 131104 | tf_op jit(solution)/shard_map/all_to_all | solution.py:102
  30.9 4.4 %all-to-all-start.3 = ((bf16[8,2,8,512]{3,2,1,0:T(8,128)(2,1)}), bf16[8,2,8,512]{3,2,1,0:T(8,128)(2,1)S(1)}, u32[]{:S(2)}, u32[]{:S(2)}) async-start(bf16[8,2,8,512]{3,2,1,0:T(8,128)(2,1)} %bitcast.23), calls=%async_computation.3 | async-start | bytes 262144 | tf_op jit(solution)/shard_map/all_to_all | solution.py:103
  35.3 0.0 all-gather.5.cloned.1.call-start
  35.3 0.6 gather_fusion.4
  35.8 5.1 %all-to-all-done.3 = bf16[8,2,8,512]{3,2,1,0:T(8,128)(2,1)S(1)} async-done(((bf16[8,2,8,512]{3,2,1,0:T(8,128)(2,1)}), bf16[8,2,8,512]{3,2,1,0:T(8,128)(2,1)S(1)}, u32[]{:S(2)}, u32[]{:S(2)}) %all-to-all-start.3) | async-done | bytes 131104 | tf_op jit(solution)/shard_map/all_to_all | solution.py:103
  41.0 0.6 gather_fusion.6
  41.5 0.8 select_bitcast_fusion
  42.3 0.0 all-gather.5.cloned.1.call-update
  42.4 0.0 all-gather.3.cloned.1.call-start
  42.4 0.7 all-gather.3.cloned.1.call-update
  43.1 0.6 gather_fusion.1
  43.7 1.1 broadcast_select_fusion.1
  44.8 4.6 %all-to-all-start = ((bf16[8,2,8,3584]{3,2,1,0:T(8,128)(2,1)}), bf16[8,2,8,3584]{3,2,1,0:T(8,128)(2,1)S(1)}, u32[]{:S(2)}, u32[]{:S(2)}) async-start(bf16[8,2,8,3584]{3,2,1,0:T(8,128)(2,1)} %bitcast.15), calls=%async_computation | async-start | bytes 1835008 | tf_op jit(solution)/shard_map/all_to_all | solution.py:101
  49.4 1.3 dynamic_slice.3
  51.3 20.2 %all-to-all-done = bf16[8,2,8,3584]{3,2,1,0:T(8,128)(2,1)S(1)} async-done(((bf16[8,2,8,3584]{3,2,1,0:T(8,128)(2,1)}), bf16[8,2,8,3584]{3,2,1,0:T(8,128)(2,1)S(1)}, u32[]{:S(2)}, u32[]{:S(2)}) %all-to-all-start) | async-done | bytes 917536 | tf_op jit(solution)/shard_map/all_to_all | solution.py:101
  71.5 0.6 gather_fusion.2
  72.2 1.1 broadcast_select_fusion
  73.2 83.6 %all-gather.5.cloned.1.call-done = bf16[4096,512]{1,0:T(8,128)(2,1)} async-done(((bf16[128,512]{1,0:T(8,128)(2,1)}), bf16[4096,512]{1,0:T(8,128)(2,1)}) %all-gather.5.cloned.1.call-update) | async-done | bytes 4194320 | tf_op jit(solution)/shard_map/all_gather | solution.py:138
  156.8 6.4 %copy.42 = bf16[4096,512]{0,1:T(8,128)(2,1)} copy(bf16[4096,512]{1,0:T(8,128)(2,1)} %all-gather.5.cloned.1.call-done) | data formatting | bytes 8388608 | tf_op jit(solution)/shard_map/all_gather | solution.py:138
  163.2 102.9 %all-gather.3.cloned.1.call-done = bf16[4096,512]{1,0:T(8,128)(2,1)} async-done(((bf16[128,512]{1,0:T(8,128)(2,1)}), bf16[4096,512]{1,0:T(8,128)(2,1)}) %all-gather.3.cloned.1.call-update) | async-done | bytes 4194320 | tf_op jit(solution)/shard_map/all_gather | solution.py:137
  266.1 6.4 %copy.41 = bf16[4096,512]{0,1:T(8,128)(2,1)} copy(bf16[4096,512]{1,0:T(8,128)(2,1)} %all-gather.3.cloned.1.call-done) | data formatting | bytes 8388608 | tf_op jit(solution)/shard_map/all_gather | solution.py:137
  272.5 42.3 %conditional.2 = (f32[4,7,64]{2,1,0:T(8,128)S(1)}, f32[64,4,7,128]{3,0,2,1:T(8,128)}) conditional(s32[]{:T(128)} %convert_element_type.23, () %tuple.23, (s32[4096]{0:T(1024)S(1)}, s32[]{:T(128)}, s32[]{:T(128)}, s32[4096]{0:T(1024)S(1)}, bf16[16,8,3584]{2,1,0:T(8,128)(2,1)}, /*index=5*/bf16[4096,4,128]{0,2,1:T(8,128)(2,1)}, ...), branch_computations={%region_3.0_spmd, %region_4.9_spmd} | conditional | flops 3839363328 | bytes 117590584 | solution.py:58
  272.6 0.2 compare_and_fusion
  272.8 1.1 slice.8
  273.9 0.6 reshape.200
  274.5 13.9 %fusion = (f32[4,7,64]{2,1,0:T(8,128)S(1)}, f32[4,4096,64,7]{1,2,3,0:T(8,128)}) fusion(pred[64,4096]{1,0:T(8,128)(4,1)S(1)} %compare_and_fusion, bf16[64,4,7,128]{3,2,1,0:T(8,128)(2,1)S(1)} %reshape.200, bf16[4096,4,128]{0,2,1:T(8,128)(2,1)} %get-tuple-element.106), kind=kOutput, calls=%fused_computation.9 | convolution fusion | flops 1901066496 | bytes 34282496 | tf_op jit(solution)/shard_map/cond/branch_1_fun/rkgd,nkd->kgrn/dot_general | solution.py:39
  288.4 12.9 %fusion.11 = f32[64,4,7,128]{3,0,2,1:T(8,128)} fusion(bf16[4096,4,128]{0,2,1:T(8,128)(2,1)S(1)} %copy-done.2, f32[4,4096,64,7]{1,2,3,0:T(8,128)} %get-tuple-element.116, f32[4,7,64]{2,1,0:T(8,128)S(1)} %broadcast_maximum_fusion, pred[64,4096]{1,0:T(8,128)(4,1)S(1)} %compare_and_fusion), kind=kOutput, calls=%fused_computation.19 | convolution fusion | flops 1908408320 | bytes 34741248 | tf_op jit(solution)/shard_map/cond/branch_1_fun/kgrn,nkd->rkgd/dot_general | solution.py:49
  301.3 13.6 %fusion.4 = f32[4,7,64]{2,1,0:T(8,128)S(1)} fusion(f32[4,4096,64,7]{1,2,3,0:T(8,128)} %get-tuple-element.116, f32[4,7,64]{2,1,0:T(8,128)S(1)} %broadcast_maximum_fusion, pred[64,4096]{1,0:T(8,128)(4,1)S(1)} %compare_and_fusion), kind=kLoop, calls=%fused_computation.13 | loop fusion | flops 29358336 | bytes 29636608 | tf_op jit(solution)/shard_map/cond/branch_1_fun/reduce_sum | solution.py:48
  314.9 1.5 broadcast_divide_fusion.1
  316.4 0.3 copy.45
  316.7 0.5 reshape.226
  317.2 0.9 select_convert_fusion.1
  318.1 42.9 %conditional.3 = (f32[4,7,64]{2,1,0:T(8,128)}, f32[64,4,7,128]{3,0,2,1:T(8,128)}) conditional(s32[]{:T(128)} %convert_element_type.26, () %tuple.25, (s32[4096]{0:T(1024)S(1)}, s32[]{:T(128)}, s32[]{:T(128)}, s32[4096]{0:T(1024)S(1)}, bf16[16,8,3584]{2,1,0:T(8,128)(2,1)}, /*index=5*/bf16[4096,4,128]{0,2,1:T(8,128)(2,1)}, ...), branch_computations={%region_7.10_spmd, %region_8.13_spmd} | conditional | flops 3839363328 | bytes 117590584 | solution.py:58
  318.2 0.2 compare_and_fusion.1
  318.4 1.1 slice.9
  319.5 0.6 reshape.201
  320.0 0.0 copy-start.3
  320.0 13.9 %fusion.19 = (f32[4,7,64]{2,1,0:T(8,128)S(1)}, f32[4,4096,64,7]{1,2,3,0:T(8,128)}) fusion(pred[64,4096]{1,0:T(8,128)(4,1)S(1)} %compare_and_fusion.1, bf16[64,4,7,128]{3,2,1,0:T(8,128)(2,1)S(1)} %reshape.201, bf16[4096,4,128]{0,2,1:T(8,128)(2,1)} %get-tuple-element.113), kind=kOutput, calls=%fused_computation.29 | convolution fusion | flops 1901066496 | bytes 34282496 | tf_op jit(solution)/shard_map/cond/branch_1_fun/rkgd,nkd->kgrn/dot_general | solution.py:39
  334.0 0.0 copy-done.3
  334.0 12.9 %fusion.30 = f32[64,4,7,128]{3,0,2,1:T(8,128)} fusion(bf16[4096,4,128]{0,2,1:T(8,128)(2,1)S(1)} %copy-done.3, f32[4,4096,64,7]{1,2,3,0:T(8,128)} %get-tuple-element.118, f32[4,7,64]{2,1,0:T(8,128)S(1)} %broadcast_maximum_fusion.1, pred[64,4096]{1,0:T(8,128)(4,1)S(1)} %compare_and_fusion.1), kind=kOutput, calls=%fused_computation.39 | convolution fusion | flops 1908408320 | bytes 34741248 | tf_op jit(solution)/shard_map/cond/branch_1_fun/kgrn,nkd->rkgd/dot_general | solution.py:49
  346.9 14.2 %fusion.23 = f32[4,7,64]{2,1,0:T(8,128)} fusion(f32[4,4096,64,7]{1,2,3,0:T(8,128)} %get-tuple-element.118, f32[4,7,64]{2,1,0:T(8,128)S(1)} %broadcast_maximum_fusion.1, pred[64,4096]{1,0:T(8,128)(4,1)S(1)} %compare_and_fusion.1), kind=kLoop, calls=%fused_computation.33 | loop fusion | flops 29358336 | bytes 29636608 | tf_op jit(solution)/shard_map/cond/branch_1_fun/reduce_sum | solution.py:48
  361.1 0.8 select_bitcast_fusion.2
  361.9 1.5 broadcast_divide_fusion
  363.4 0.3 copy.48
  363.7 0.5 reshape.227
  364.2 0.1 select_convert_fusion
  364.3 2.0 maximum_bitcast_fusion
  (25 shorter events, 0.1 us)
Async XLA Ops:
  6.5 36.6 %copy-start = (bf16[1,16,8,3584]{3,2,1,0:T(8,128)(2,1)S(1)}, bf16[1,16,8,3584]{3,2,1,0:T(8,128)(2,1)}, u32[]{:S(2)}) copy-start(bf16[1,16,8,3584]{3,2,1,0:T(8,128)(2,1)} %param.14) | copy-start | bytes 2752516
  10.3 10.1 %all-to-all-start.1 = ((s32[8,1,2]{2,1,0:T(1,128)}), s32[8,1,2]{2,1,0:T(1,128)S(1)}, u32[]{:S(2)}, u32[]{:S(2)}) async-start(s32[8,1,2]{2,1,0:T(1,128)} %bitcast.13), calls=%async_computation.1 | async-start | bytes 8192 | tf_op jit(solution)/shard_map/all_to_all | solution.py:104
  20.4 10.4 %all-to-all-start.2 = ((bf16[8,2,8,512]{3,2,1,0:T(8,128)(2,1)}), bf16[8,2,8,512]{3,2,1,0:T(8,128)(2,1)S(1)}, u32[]{:S(2)}, u32[]{:S(2)}) async-start(bf16[8,2,8,512]{3,2,1,0:T(8,128)(2,1)} %bitcast.18), calls=%async_computation.2 | async-start | bytes 262144 | tf_op jit(solution)/shard_map/all_to_all | solution.py:102
  30.9 10.1 %all-to-all-start.3 = ((bf16[8,2,8,512]{3,2,1,0:T(8,128)(2,1)}), bf16[8,2,8,512]{3,2,1,0:T(8,128)(2,1)S(1)}, u32[]{:S(2)}, u32[]{:S(2)}) async-start(bf16[8,2,8,512]{3,2,1,0:T(8,128)(2,1)} %bitcast.23), calls=%async_computation.3 | async-start | bytes 262144 | tf_op jit(solution)/shard_map/all_to_all | solution.py:103
  35.3 121.5 %all-gather.5.cloned.1.call-start = ((), (), s32[]{:S(2)}) async-start(), calls=%async_computation.5 | async-start | bytes 4325376 | tf_op jit(solution)/shard_map/all_gather | solution.py:138
  42.4 223.7 %all-gather.3.cloned.1.call-start = ((), (), s32[]{:S(2)}) async-start(), calls=%async_computation.4 | async-start | bytes 4325376 | tf_op jit(solution)/shard_map/all_gather | solution.py:137
  44.8 26.7 %all-to-all-start = ((bf16[8,2,8,3584]{3,2,1,0:T(8,128)(2,1)}), bf16[8,2,8,3584]{3,2,1,0:T(8,128)(2,1)S(1)}, u32[]{:S(2)}, u32[]{:S(2)}) async-start(bf16[8,2,8,3584]{3,2,1,0:T(8,128)(2,1)} %bitcast.15), calls=%async_computation | async-start | bytes 1835008 | tf_op jit(solution)/shard_map/all_to_all | solution.py:101
  274.4 14.0 %copy-start.2 = (bf16[4096,4,128]{0,2,1:T(8,128)(2,1)S(1)}, bf16[4096,4,128]{0,2,1:T(8,128)(2,1)}, u32[]{:S(2)}) copy-start(bf16[4096,4,128]{0,2,1:T(8,128)(2,1)} %get-tuple-element.107) | copy-start | bytes 12582916 | tf_op jit(solution)/shard_map/cond
  320.0 14.0 %copy-start.3 = (bf16[4096,4,128]{0,2,1:T(8,128)(2,1)S(1)}, bf16[4096,4,128]{0,2,1:T(8,128)(2,1)}, u32[]{:S(2)}) copy-start(bf16[4096,4,128]{0,2,1:T(8,128)(2,1)} %get-tuple-element.114) | copy-start | bytes 12582916 | tf_op jit(solution)/shard_map/cond
  361.1 5.3 %copy-start.1 = (bf16[1,16,8,3584]{3,2,1,0:T(8,128)(2,1)S(1)}, bf16[1,16,8,3584]{3,2,1,0:T(8,128)(2,1)}, u32[]{:S(2)}) copy-start(bf16[1,16,8,3584]{3,2,1,0:T(8,128)(2,1)} %param.14) | copy-start | bytes 2752516
Sparse Core Ops, SparseCore 0:
  42.5 114.2 all-gather.4
  160.3 105.7 all-gather.2
where the time goes:
time: 374 us; the launch traced here: 373 us
  waiting for transfers between devices  217 us (58%)
  matrix products  53.7 us (14%)
  other arithmetic  41.9 us (11%)
  local copies, waits for them, and re-layouts  26.4 us (7%)
  starting transfers between devices  19.8 us (5%)
  between operations  14.2 us (4%)
    all_gather x1, waiting for transfers between devices, local(): lax.all_gather(local_k, 'ctx', axis=0, tiled=True)  103 us
    all_gather x1, waiting for transfers between devices, local(): lax.all_gather(local_v, 'ctx', axis=0, tiled=True)  83.6 us
    dot_general x2, matrix products, advance(): jnp.einsum('rkgd,nkd->kgrn', queries, key_rows, preferred_element_type=jn...  27.9 us
    reduce_sum x2, other arithmetic, advance(): weight_sum = jnp.sum(weights, axis=-1)  27.7 us
    dot_general x2, matrix products, advance(): jnp.einsum('kgrn,nkd->rkgd', weights.astype(jnp.bfloat16), value_rows, pr...  25.8 us
    all_to_all x1, waiting for transfers between devices, local(): lax.all_to_all(send_q, 'sec', split_axis=0, concat_axis=0, tiled=True)  20.2 us
  transfers between devices with their start and end apart: 6, of which 6 were waited for; matrix products, arithmetic and copies ran while one was open for 4% of the time, Pallas kernels for 0%

commit v1 on v0

--- a/solution.py
+++ b/solution.py
@@ -134,7 +134,9 @@
     states = absorb(
         (empty_state, empty_state),
         (
-            lax.all_gather(local_k, "ctx", axis=0, tiled=True),
+            jnp.concatenate(
+                lax.all_to_all(jnp.stack([local_k] * lax.axis_size("ctx")), "ctx", 0, 0), axis=0
+            ),
             lax.all_gather(local_v, "ctx", axis=0, tiled=True),
         ),
         jnp.int32(0),

time: 374 us -> 347 us (0.928)
  waiting for transfers between devices: 217 us -> 164 us
  starting transfers between devices: 19.8 us -> 31.2 us
  local copies, waits for them, and re-layouts: 26.4 us -> 37.1 us
    all_gather x1 -> x0, waiting for transfers between devices: 103 us -> none  [local(): lax.all_gather(local_k, 'ctx', axis=0, tiled=True)]
    all_gather x1, waiting for transfers between devices: 83.6 us -> 136 us  [local(): lax.all_gather(local_v, 'ctx', axis=0, tiled=True)]
    all_to_all x0 -> x1, starting transfers between devices: none -> 11.5 us  [local(): lax.all_to_all(jnp.stack([local_k] * lax.axis_size('ctx')), 'ctx', 0, 0)]
    another operation x0 -> x3, local copies, waits for them, and re-layouts: none -> 10.3 us  [the longest x1 7.32 us: absorb(): key_rows = key_block.reshape(key_count, kv_heads, head_dim)]
    all_to_all x0 -> x1, local copies, waits for them, and re-layouts: none -> 6.86 us  [local(): lax.all_to_all(jnp.stack([local_k] * lax.axis_size('ctx')), 'ctx', 0, 0)]
    all_gather x1 -> x0, local copies, waits for them, and re-layouts: 6.43 us -> none  [local(): lax.all_gather(local_k, 'ctx', axis=0, tiled=True)]
  transfers between devices with their start and end apart: 6 -> 6, of which waited for: 6 -> 5; matrix products, arithmetic and copies ran while one was open for 4% -> 6% of each run, Pallas kernels for 0% -> 0%
where the time goes in v1:
time: 347 us; the launch traced here: 343 us
  waiting for transfers between devices  164 us (47%)
  matrix products  53.7 us (15%)
  other arithmetic  41.9 us (12%)
  local copies, waits for them, and re-layouts  37.1 us (11%)
  starting transfers between devices  31.2 us (9%)
  between operations  14.2 us (4%)
    all_gather x1, waiting for transfers between devices, local(): lax.all_gather(local_v, 'ctx', axis=0, tiled=True)  136 us
    dot_general x2, matrix products, advance(): jnp.einsum('rkgd,nkd->kgrn', queries, key_rows, preferred_element_type=jn...  27.9 us
    reduce_sum x2, other arithmetic, advance(): weight_sum = jnp.sum(weights, axis=-1)  27.7 us
    dot_general x2, matrix products, advance(): jnp.einsum('kgrn,nkd->rkgd', weights.astype(jnp.bfloat16), value_rows, pr...  25.8 us
    all_to_all x1, waiting for transfers between devices, local(): lax.all_to_all(send_q, 'sec', split_axis=0, concat_axis=0, tiled=True)  17.8 us
    all_to_all x1, starting transfers between devices, local(): lax.all_to_all(jnp.stack([local_k] * lax.axis_size('ctx')), 'ctx', 0, 0)  11.5 us
    another operation x1, local copies, waits for them, and re-layouts, absorb(): key_rows = key_block.reshape(key_count, kv_heads, head_dim)  7.32 us
  transfers between devices with their start and end apart: 6, of which 5 were waited for; matrix products, arithmetic and copies ran while one was open for 6% of the time, Pallas kernels for 0%

profile of v1, /device:TPU:32, one launch (start us, length us, event | category | flops | bytes accessed | tf_op | source)
XLA Modules:
  0.0 342.6 jit_solution(9119488164202849220)
XLA Ops:
  6.5 0.9 convert_reduce_fusion
  7.5 0.7 multiply_add_fusion
  8.1 0.1 select_reduce_fusion.1
  8.2 0.1 reduce_sum.51
  8.3 1.3 gather_fusion
  9.6 0.1 gather.13
  9.7 0.6 and_select_fusion
  10.3 6.0 %all-to-all-start.1 = ((s32[8,1,2]{2,1,0:T(1,128)}), s32[8,1,2]{2,1,0:T(1,128)S(1)}, u32[]{:S(2)}, u32[]{:S(2)}) async-start(s32[8,1,2]{2,1,0:T(1,128)} %bitcast.13), calls=%async_computation.1 | async-start | bytes 8192 | tf_op jit(solution)/shard_map/all_to_all | solution.py:104
  16.4 1.5 gather_fusion.5
  17.8 1.5 gather_fusion.3
  19.3 0.8 broadcast_select_fusion.2
  20.1 0.3 all-to-all-done.1
  20.4 4.8 %all-to-all-start.2 = ((bf16[8,2,8,512]{3,2,1,0:T(8,128)(2,1)}), bf16[8,2,8,512]{3,2,1,0:T(8,128)(2,1)S(1)}, u32[]{:S(2)}, u32[]{:S(2)}) async-start(bf16[8,2,8,512]{3,2,1,0:T(8,128)(2,1)} %bitcast.18), calls=%async_computation.2 | async-start | bytes 262144 | tf_op jit(solution)/shard_map/all_to_all | solution.py:102
  25.2 0.6 gather_fusion.1
  25.8 5.1 %all-to-all-done.2 = bf16[8,2,8,512]{3,2,1,0:T(8,128)(2,1)S(1)} async-done(((bf16[8,2,8,512]{3,2,1,0:T(8,128)(2,1)}), bf16[8,2,8,512]{3,2,1,0:T(8,128)(2,1)S(1)}, u32[]{:S(2)}, u32[]{:S(2)}) %all-to-all-start.2) | async-done | bytes 131104 | tf_op jit(solution)/shard_map/all_to_all | solution.py:102
  30.9 4.4 %all-to-all-start.4 = ((bf16[8,2,8,512]{3,2,1,0:T(8,128)(2,1)}), bf16[8,2,8,512]{3,2,1,0:T(8,128)(2,1)S(1)}, u32[]{:S(2)}, u32[]{:S(2)}) async-start(bf16[8,2,8,512]{3,2,1,0:T(8,128)(2,1)} %bitcast.22), calls=%async_computation.4 | async-start | bytes 262144 | tf_op jit(solution)/shard_map/all_to_all | solution.py:103
  35.3 1.1 broadcast_select_fusion.1
  36.3 4.6 %all-to-all-done.4 = bf16[8,2,8,512]{3,2,1,0:T(8,128)(2,1)S(1)} async-done(((bf16[8,2,8,512]{3,2,1,0:T(8,128)(2,1)}), bf16[8,2,8,512]{3,2,1,0:T(8,128)(2,1)S(1)}, u32[]{:S(2)}, u32[]{:S(2)}) %all-to-all-start.4) | async-done | bytes 131104 | tf_op jit(solution)/shard_map/all_to_all | solution.py:103
  41.0 4.6 %all-to-all-start = ((bf16[8,2,8,3584]{3,2,1,0:T(8,128)(2,1)}), bf16[8,2,8,3584]{3,2,1,0:T(8,128)(2,1)S(1)}, u32[]{:S(2)}, u32[]{:S(2)}) async-start(bf16[8,2,8,3584]{3,2,1,0:T(8,128)(2,1)} %bitcast.15), calls=%async_computation | async-start | bytes 1835008 | tf_op jit(solution)/shard_map/all_to_all | solution.py:101
  45.5 0.6 broadcast.298
  46.1 0.6 reduce.3
  46.8 0.1 reshape.213
  46.9 0.1 select_reduce_fusion
  47.0 0.6 gather_fusion.4
  47.6 0.6 gather_fusion.6
  48.1 0.7 select_bitcast_fusion
  48.9 0.0 all-gather.2.cloned.1.call-update
  48.9 0.1 copy.43
  49.0 17.8 %all-to-all-done = bf16[8,2,8,3584]{3,2,1,0:T(8,128)(2,1)S(1)} async-done(((bf16[8,2,8,3584]{3,2,1,0:T(8,128)(2,1)}), bf16[8,2,8,3584]{3,2,1,0:T(8,128)(2,1)S(1)}, u32[]{:S(2)}, u32[]{:S(2)}) %all-to-all-start) | async-done | bytes 917536 | tf_op jit(solution)/shard_map/all_to_all | solution.py:101
  66.8 2.9 stack.3
  69.7 11.5 %all-to-all-start.3 = ((bf16[32,128,512]{1,2,0:T(8,128)(2,1)}), bf16[32,128,512]{1,2,0:T(8,128)(2,1)}, u32[]{:S(2)}, u32[]{:S(2)}) async-start(bf16[32,128,512]{1,2,0:T(8,128)(2,1)} %stack.3), calls=%async_computation.3 | async-start | bytes 8388608 | tf_op jit(solution)/shard_map/all_to_all | solution.py:138
  81.2 1.2 dynamic_slice.3
  83.1 0.6 gather_fusion.2
  83.7 1.1 broadcast_select_fusion
  84.8 136.3 %all-gather.2.cloned.1.call-done = bf16[4096,512]{1,0:T(8,128)(2,1)} async-done(((bf16[128,512]{1,0:T(8,128)(2,1)}), bf16[4096,512]{1,0:T(8,128)(2,1)}) %all-gather.2.cloned.1.call-update) | async-done | bytes 4194320 | tf_op jit(solution)/shard_map/all_gather | solution.py:140
  221.1 6.4 %copy.45 = bf16[4096,512]{0,1:T(8,128)(2,1)} copy(bf16[4096,512]{1,0:T(8,128)(2,1)} %all-gather.2.cloned.1.call-done) | data formatting | bytes 8388608 | tf_op jit(solution)/shard_map/all_gather | solution.py:140
  227.5 0.0 all-to-all-done.3
  227.5 6.9 %copy.44 = bf16[32,128,512]{1,0,2:T(8,128)(2,1)} copy(bf16[32,128,512]{1,2,0:T(8,128)(2,1)} %all-to-all-done.3) | data formatting | bytes 8388608 | tf_op jit(solution)/shard_map/all_to_all | solution.py:138
  234.4 7.3 %reshape_reshape.3 = bf16[4096,4,128]{0,2,1:T(8,128)(2,1)} reshape(bf16[32,128,512]{1,0,2:T(8,128)(2,1)} %copy.44) | data formatting | bytes 8388608 | tf_op jit(solution)/shard_map/reshape;reshape | solution.py:24
  241.7 42.6 %conditional.2 = (f32[4,7,64]{2,1,0:T(8,128)S(1)}, f32[64,4,7,128]{3,0,2,1:T(8,128)}) conditional(s32[]{:T(128)} %convert_element_type.23, () %tuple.23, (s32[4096]{0:T(1024)S(1)}, s32[]{:T(128)}, s32[]{:T(128)}, s32[4096]{0:T(1024)S(1)}, bf16[16,8,3584]{2,1,0:T(8,128)(2,1)}, /*index=5*/bf16[4096,4,128]{0,2,1:T(8,128)(2,1)}, ...), branch_computations={%region_3.0_spmd, %region_4.9_spmd} | conditional | flops 3839363328 | bytes 117590584 | solution.py:58
  241.9 0.2 compare_and_fusion
  242.2 1.1 slice.8
  243.2 0.6 reshape.198
  243.8 14.0 %fusion = (f32[4,7,64]{2,1,0:T(8,128)S(1)}, f32[4,4096,64,7]{1,2,3,0:T(8,128)}) fusion(pred[64,4096]{1,0:T(8,128)(4,1)S(1)} %compare_and_fusion, bf16[64,4,7,128]{3,2,1,0:T(8,128)(2,1)S(1)} %reshape.198, bf16[4096,4,128]{0,2,1:T(8,128)(2,1)} %get-tuple-element.106), kind=kOutput, calls=%fused_computation.9 | convolution fusion | flops 1901066496 | bytes 34282496 | tf_op jit(solution)/shard_map/cond/branch_1_fun/rkgd,nkd->kgrn/dot_general | solution.py:39
  257.8 0.0 copy-done.2
  257.8 12.9 %fusion.11 = f32[64,4,7,128]{3,0,2,1:T(8,128)} fusion(bf16[4096,4,128]{0,2,1:T(8,128)(2,1)S(1)} %copy-done.2, f32[4,4096,64,7]{1,2,3,0:T(8,128)} %get-tuple-element.116, f32[4,7,64]{2,1,0:T(8,128)S(1)} %broadcast_maximum_fusion, pred[64,4096]{1,0:T(8,128)(4,1)S(1)} %compare_and_fusion), kind=kOutput, calls=%fused_computation.19 | convolution fusion | flops 1908408320 | bytes 34741248 | tf_op jit(solution)/shard_map/cond/branch_1_fun/kgrn,nkd->rkgd/dot_general | solution.py:49
  270.7 13.6 %fusion.4 = f32[4,7,64]{2,1,0:T(8,128)S(1)} fusion(f32[4,4096,64,7]{1,2,3,0:T(8,128)} %get-tuple-element.116, f32[4,7,64]{2,1,0:T(8,128)S(1)} %broadcast_maximum_fusion, pred[64,4096]{1,0:T(8,128)(4,1)S(1)} %compare_and_fusion), kind=kLoop, calls=%fused_computation.13 | loop fusion | flops 29358336 | bytes 29636608 | tf_op jit(solution)/shard_map/cond/branch_1_fun/reduce_sum | solution.py:48
  284.3 1.5 broadcast_divide_fusion.1
  285.8 0.3 copy.48
  286.1 0.5 reshape.220
  286.6 0.9 select_convert_fusion.1
  287.5 42.9 %conditional.3 = (f32[4,7,64]{2,1,0:T(8,128)}, f32[64,4,7,128]{3,0,2,1:T(8,128)}) conditional(s32[]{:T(128)} %convert_element_type.26, () %tuple.25, (s32[4096]{0:T(1024)S(1)}, s32[]{:T(128)}, s32[]{:T(128)}, s32[4096]{0:T(1024)S(1)}, bf16[16,8,3584]{2,1,0:T(8,128)(2,1)}, /*index=5*/bf16[4096,4,128]{0,2,1:T(8,128)(2,1)}, ...), branch_computations={%region_7.10_spmd, %region_8.13_spmd} | conditional | flops 3839363328 | bytes 117590584 | solution.py:58
  287.5 0.2 compare_and_fusion.1
  287.8 1.1 slice.9
  288.8 0.6 reshape.199
  289.4 14.0 %fusion.19 = (f32[4,7,64]{2,1,0:T(8,128)S(1)}, f32[4,4096,64,7]{1,2,3,0:T(8,128)}) fusion(pred[64,4096]{1,0:T(8,128)(4,1)S(1)} %compare_and_fusion.1, bf16[64,4,7,128]{3,2,1,0:T(8,128)(2,1)S(1)} %reshape.199, bf16[4096,4,128]{0,2,1:T(8,128)(2,1)} %get-tuple-element.113), kind=kOutput, calls=%fused_computation.29 | convolution fusion | flops 1901066496 | bytes 34282496 | tf_op jit(solution)/shard_map/cond/branch_1_fun/rkgd,nkd->kgrn/dot_general | solution.py:39
  303.4 12.9 %fusion.30 = f32[64,4,7,128]{3,0,2,1:T(8,128)} fusion(bf16[4096,4,128]{0,2,1:T(8,128)(2,1)S(1)} %copy-done.3, f32[4,4096,64,7]{1,2,3,0:T(8,128)} %get-tuple-element.118, f32[4,7,64]{2,1,0:T(8,128)S(1)} %broadcast_maximum_fusion.1, pred[64,4096]{1,0:T(8,128)(4,1)S(1)} %compare_and_fusion.1), kind=kOutput, calls=%fused_computation.39 | convolution fusion | flops 1908408320 | bytes 34741248 | tf_op jit(solution)/shard_map/cond/branch_1_fun/kgrn,nkd->rkgd/dot_general | solution.py:49
  316.3 14.2 %fusion.23 = f32[4,7,64]{2,1,0:T(8,128)} fusion(f32[4,4096,64,7]{1,2,3,0:T(8,128)} %get-tuple-element.118, f32[4,7,64]{2,1,0:T(8,128)S(1)} %broadcast_maximum_fusion.1, pred[64,4096]{1,0:T(8,128)(4,1)S(1)} %compare_and_fusion.1), kind=kLoop, calls=%fused_computation.33 | loop fusion | flops 29358336 | bytes 29636608 | tf_op jit(solution)/shard_map/cond/branch_1_fun/reduce_sum | solution.py:48
  330.5 0.8 select_bitcast_fusion.2
  331.3 1.5 broadcast_divide_fusion
  332.8 0.3 copy.51
  333.1 0.5 reshape.221
  333.6 0.1 select_convert_fusion
  333.7 2.0 maximum_bitcast_fusion
  (27 shorter events, 0.1 us)
Async XLA Ops:
  6.5 18.7 %copy-start = (bf16[1,16,8,3584]{3,2,1,0:T(8,128)(2,1)S(1)}, bf16[1,16,8,3584]{3,2,1,0:T(8,128)(2,1)}, u32[]{:S(2)}) copy-start(bf16[1,16,8,3584]{3,2,1,0:T(8,128)(2,1)} %param.14) | copy-start | bytes 2752516
  10.3 10.1 %all-to-all-start.1 = ((s32[8,1,2]{2,1,0:T(1,128)}), s32[8,1,2]{2,1,0:T(1,128)S(1)}, u32[]{:S(2)}, u32[]{:S(2)}) async-start(s32[8,1,2]{2,1,0:T(1,128)} %bitcast.13), calls=%async_computation.1 | async-start | bytes 8192 | tf_op jit(solution)/shard_map/all_to_all | solution.py:104
  20.4 10.4 %all-to-all-start.2 = ((bf16[8,2,8,512]{3,2,1,0:T(8,128)(2,1)}), bf16[8,2,8,512]{3,2,1,0:T(8,128)(2,1)S(1)}, u32[]{:S(2)}, u32[]{:S(2)}) async-start(bf16[8,2,8,512]{3,2,1,0:T(8,128)(2,1)} %bitcast.18), calls=%async_computation.2 | async-start | bytes 262144 | tf_op jit(solution)/shard_map/all_to_all | solution.py:102
  30.9 10.1 %all-to-all-start.4 = ((bf16[8,2,8,512]{3,2,1,0:T(8,128)(2,1)}), bf16[8,2,8,512]{3,2,1,0:T(8,128)(2,1)S(1)}, u32[]{:S(2)}, u32[]{:S(2)}) async-start(bf16[8,2,8,512]{3,2,1,0:T(8,128)(2,1)} %bitcast.22), calls=%async_computation.4 | async-start | bytes 262144 | tf_op jit(solution)/shard_map/all_to_all | solution.py:103
  41.0 25.8 %all-to-all-start = ((bf16[8,2,8,3584]{3,2,1,0:T(8,128)(2,1)}), bf16[8,2,8,3584]{3,2,1,0:T(8,128)(2,1)S(1)}, u32[]{:S(2)}, u32[]{:S(2)}) async-start(bf16[8,2,8,3584]{3,2,1,0:T(8,128)(2,1)} %bitcast.15), calls=%async_computation | async-start | bytes 1835008 | tf_op jit(solution)/shard_map/all_to_all | solution.py:101
  45.5 175.6 %all-gather.2.cloned.1.call-start = ((), (), s32[]{:S(2)}) async-start(), calls=%async_computation.5 | async-start | bytes 4325376 | tf_op jit(solution)/shard_map/all_gather | solution.py:140
  69.7 157.8 %all-to-all-start.3 = ((bf16[32,128,512]{1,2,0:T(8,128)(2,1)}), bf16[32,128,512]{1,2,0:T(8,128)(2,1)}, u32[]{:S(2)}, u32[]{:S(2)}) async-start(bf16[32,128,512]{1,2,0:T(8,128)(2,1)} %stack.3), calls=%async_computation.3 | async-start | bytes 8388608 | tf_op jit(solution)/shard_map/all_to_all | solution.py:138
  243.8 14.0 %copy-start.2 = (bf16[4096,4,128]{0,2,1:T(8,128)(2,1)S(1)}, bf16[4096,4,128]{0,2,1:T(8,128)(2,1)}, u32[]{:S(2)}) copy-start(bf16[4096,4,128]{0,2,1:T(8,128)(2,1)} %get-tuple-element.107) | copy-start | bytes 12582916 | tf_op jit(solution)/shard_map/cond
  289.4 14.0 %copy-start.3 = (bf16[4096,4,128]{0,2,1:T(8,128)(2,1)S(1)}, bf16[4096,4,128]{0,2,1:T(8,128)(2,1)}, u32[]{:S(2)}) copy-start(bf16[4096,4,128]{0,2,1:T(8,128)(2,1)} %get-tuple-element.114) | copy-start | bytes 12582916 | tf_op jit(solution)/shard_map/cond
  330.5 5.3 %copy-start.1 = (bf16[1,16,8,3584]{3,2,1,0:T(8,128)(2,1)S(1)}, bf16[1,16,8,3584]{3,2,1,0:T(8,128)(2,1)}, u32[]{:S(2)}) copy-start(bf16[1,16,8,3584]{3,2,1,0:T(8,128)(2,1)} %param.14) | copy-start | bytes 2752516
Sparse Core Ops, SparseCore 0:
  49.9 171.1 all-gather.1
